TPU v7x, 32 devices: a whole 2x2x4 slice. The times are simulated.
32 devices in a mesh: parts: 2 (over y), seq: 4 (over z), head: 4 (over x, core).
Axes of the slice: x: 2, y: 2, z: 4, core: 2. Of those that a mesh axis runs over, the one named last changes fastest.
Arguments:
- query_rows: bfloat16 [6144, 4096], P(('parts', 'seq', 'head')), parts along dimension 0, may hold values from -12 to 12
- key_rows: bfloat16 [6144, 4096], P(('parts', 'seq', 'head')), parts along dimension 0, may hold values from -12 to 12
- value_rows: bfloat16 [6144, 4096], P(('parts', 'seq', 'head')), parts along dimension 0, may hold values from -6 to 6
- block_lists: int32 [64, 4, 4, 3], P('parts', 'seq'), parts along dimension 0, may hold values from 0 to 5, as said below
- block_counts: int32 [64, 4, 4], P('parts'), parts along dimension 0, may hold values from 0 to 3, as said below
Outputs:
- attended: bfloat16 [6144, 4096], P(('parts', 'seq', 'head')), parts along dimension 0
There are 2 independent parts, one for each index of `parts`. A program takes and returns all parts, laid end to end along the dimension named above; each array names one. Nothing has to cross between parts.
Inputs may be any that keep to these rules, and one draw needn't show every extreme that they name: `block_lists`: for one head, query tile and key tile the 3 entries are distinct block numbers of the key tile; only the first block_counts of them are listed. `block_counts`: 0 where the key tile is the query tile; some entries of every draw equal 3; for every k, query tile and key tile, the counts of heads 2k and 2k+1 sum to at most 4, and exactly 4 for some k in every draw.
All inputs are finite; a program needn't handle non-finite values.
Results may differ from a plain program's by a relative error of at most 0.0034.
Values may be sent and summed in bfloat16 or wider, within the bound.
A program may use at most 64 MiB of HBM per device.

v0:
```python
import functools
import math

import jax
import jax.numpy as jnp
from jax import lax
from jax.experimental import pallas as pl
from jax.experimental.pallas import tpu as pltpu
from jax.sharding import PartitionSpec as P

HEADS = 32
DH = 128
BLOCK = 128
MOST = 3
PAIR_MOST = 4
TILE = 768
MESH = pl.DeviceIdType.MESH


def contract_last(a, b):
    return lax.dot_general(a, b, (((1,), (1,)), ((), ())), preferred_element_type=jnp.float32)


def body(dims, lists_ref, q_ref, k_ref, v_ref, out_ref, *scratch):
    H, S, rows, heads, piece = dims
    pairs = heads // 2
    chips = H // 2
    kb, vb, qb = scratch[:pairs], scratch[pairs : 2 * pairs], scratch[2 * pairs : 3 * pairs]
    (ob, pk, fk, lbuf, lsm, own_lists, x_send, x_recv, z_send, z_recv, l_send, l_recv, l_loc, o_send, o_recv) = (
        scratch[3 * pairs :]
    )
    me = lax.axis_index("head")
    tile = lax.axis_index("seq")

    def peer_of(i):
        chip = lax.rem(lax.div(me, 2) + 1 + lax.div(i, 2), chips)
        return chip * 2 + lax.rem(me + i + 1, 2)

    def source_of(i):
        chip = lax.rem(lax.div(me, 2) + 2 * chips - 1 - lax.div(i, 2), chips)
        return chip * 2 + lax.rem(me + i + 1, 2)

    def tile_after(d):
        return lax.rem(tile + d, S)

    def i32(i):
        return jnp.int32(i)

    barrier = pltpu.get_barrier_semaphore()
    for i in range(H - 1):
        pl.semaphore_signal(barrier, inc=1, device_id={"head": peer_of(i32(i))}, device_id_type=MESH)
    for d in range(1, S):
        pl.semaphore_signal(barrier, inc=1, device_id={"seq": tile_after(d)}, device_id_type=MESH)

    sources = (k_ref, v_ref, q_ref)
    places = (kb, vb, qb)

    def pair_columns(owner, p):
        return pl.ds(pl.multiple_of((owner * heads + 2 * p) * DH, 2 * DH), 2 * DH)

    def row_range(owner):
        return pl.ds(pl.multiple_of(owner * rows, 16), rows)

    def source_at(a, owner, p):
        columns = pair_columns(owner, p)
        return sources[a].at[:, columns] if a == 2 else sources[a].at[:, :, columns]

    def place_at(a, owner, p):
        if a == 2:
            return places[a][p].at[row_range(owner), :]
        return places[a][p].at[pl.ds(owner * (rows // piece), rows // piece)]

    def own_copy(a, p):
        return pltpu.make_async_copy(
            source_at(a, me, p),
            place_at(a, me, p),
            x_recv.at[a, p, H - 1],
        )

    def x_copy(a, p, i, landed):
        to = peer_of(i32(i))
        at = source_of(i32(i)) if landed else me
        return pltpu.make_async_remote_copy(
            src_ref=source_at(a, to, p),
            dst_ref=place_at(a, at, p),
            send_sem=x_send.at[a, p, i],
            recv_sem=x_recv.at[a, p, i],
            device_id={"head": to},
            device_id_type=MESH,
        )

    def l_copy(d):
        to = tile_after(d)
        return pltpu.make_async_remote_copy(
            src_ref=lists_ref.at[to],
            dst_ref=lbuf.at[d - 1],
            send_sem=l_send.at[d - 1],
            recv_sem=l_recv.at[d - 1],
            device_id={"seq": to},
            device_id_type=MESH,
        )

    def z_copy(p, d, c):
        return pltpu.make_async_remote_copy(
            src_ref=pk.at[p, d - 1, c],
            dst_ref=fk.at[p, d - 1, c],
            send_sem=z_send.at[p, d - 1, c],
            recv_sem=z_recv.at[p, d - 1, c],
            device_id={"seq": tile_after(d)},
            device_id_type=MESH,
        )

    def o_copy(p, i, landed):
        to = peer_of(i)
        at = source_of(i) if landed else me
        return pltpu.make_async_remote_copy(
            src_ref=ob.at[p, i],
            dst_ref=out_ref.at[:, pair_columns(at, p)],
            send_sem=o_send.at[p, i],
            recv_sem=o_recv.at[p, i],
            device_id={"head": to},
            device_id_type=MESH,
        )

    def o_own(p):
        return pltpu.make_async_copy(
            ob.at[p, H - 1], out_ref.at[:, pair_columns(me, p)], o_recv.at[p, H - 1]
        )

    own_scalars = pltpu.make_async_copy(lists_ref, own_lists, l_loc.at[1])
    own_scalars.start()
    pl.semaphore_wait(barrier, H - 1 + S - 1)
    for d in range(1, S):
        l_copy(d).start()
    for p in range(pairs):
        for a in (0, 1):
            for i in range(H - 1):
                x_copy(a, p, i, False).start()
            own_copy(a, p).start()
    for p in range(pairs):
        for i in range(H - 1):
            x_copy(2, p, i, False).start()
        own_copy(2, p).start()

    for d in range(1, S):
        l_copy(d).wait_recv()
    to_scalars = pltpu.make_async_copy(lbuf, lsm, l_loc.at[0])
    to_scalars.start()
    to_scalars.wait()

    def arrived(a, p):
        own_copy(a, p).wait()
        for i in range(H - 1):
            x_copy(a, p, i, True).wait_recv()

    own_scalars.wait()

    def count_of(head_slot, query_tile, key_tile):
        return own_lists[key_tile, 0, heads * MOST + head_slot]

    for p in range(pairs):
        for c, held in enumerate((kb[p], vb[p])):
            arrived(c, p)
            for d in range(1, S):
                first = lsm[S - d - 1, 0, heads * MOST + 2 * p]
                for s in range(PAIR_MOST):
                    left = lsm[S - d - 1, 0, 2 * p * MOST + min(s, MOST - 1)]
                    right = lsm[S - d - 1, 0, (2 * p + 1) * MOST + min(PAIR_MOST - 1 - s, MOST - 1)]
                    for b in range(BLOCK // piece):
                        if s < PAIR_MOST - 1:
                            chosen = held[left * (BLOCK // piece) + b, :, :DH]
                        if s > 0:
                            other = held[right * (BLOCK // piece) + b, :, DH:]
                            if s < PAIR_MOST - 1:
                                chosen = jnp.where(s < first, chosen, other)
                            else:
                                chosen = other
                        pk[p, d - 1, c, s, pl.ds(b * piece, piece), :] = chosen
                z_copy(p, d, c).start()

    factor = math.log2(math.e) / math.sqrt(DH)
    width = MOST * BLOCK
    lane = lax.broadcasted_iota(jnp.int32, (1, width), 1)
    for p in range(pairs):
        arrived(2, p)
        for d in range(1, S):
            for c in range(2):
                z_copy(p, d, c).wait_recv()

        def chunk(i, carry, p=p):
            mine = row_range(peer_of(i))
            for hs in range(2):
                cols = slice(hs * DH, (hs + 1) * DH)
                q = qb[p][mine, cols]
                scores = [contract_last(q, kb[p][:, :, cols].reshape(TILE, DH))]
                values = [vb[p][:, :, cols].reshape(TILE, DH)]
                for d in range(1, S):
                    used = count_of(2 * p + hs, tile, lax.rem(tile + S - d, S)) * BLOCK
                    live = lane < used if hs == 0 else lane >= width - used
                    bias = jnp.where(live, 0.0, -jnp.inf).astype(jnp.float32)
                    far = fk[p, d - 1, 0, hs : hs + MOST].reshape(width, DH)
                    scores.append(contract_last(q, far) + bias)
                    values.append(fk[p, d - 1, 1, hs : hs + MOST].reshape(width, DH))
                top = functools.reduce(
                    jnp.maximum, [jnp.max(s, axis=1, keepdims=True) for s in scores]
                )
                total = jnp.zeros((rows, 1), jnp.float32)
                mixed = jnp.zeros((rows, DH), jnp.float32)
                for s, v in zip(scores, values):
                    w = jnp.exp2((s - top) * factor)
                    total = total + jnp.sum(w, axis=1, keepdims=True)
                    mixed = mixed + jnp.dot(
                        w.astype(jnp.bfloat16), v, preferred_element_type=jnp.float32
                    )
                ob[p, i, :, cols] = (mixed / total).astype(jnp.bfloat16)

            @pl.when(i < H - 1)
            def _():
                o_copy(p, i, False).start()

            return carry

        lax.fori_loop(0, H, chunk, 0)
        o_own(p).start()

    for p in range(pairs):
        o_own(p).wait()
        for i in range(H - 1):
            o_copy(p, i32(i), True).wait_recv()
    for d in range(1, S):
        l_copy(d).wait_send()
        for p in range(pairs):
            for c in range(2):
                z_copy(p, d, c).wait_send()
    for p in range(pairs):
        for i in range(H - 1):
            for a in range(3):
                x_copy(a, p, i, False).wait_send()
            o_copy(p, i32(i), False).wait_send()


def on_device(query_rows, key_rows, value_rows, block_lists, block_counts):
    H = lax.axis_size("head")
    S = lax.axis_size("seq")
    me = lax.axis_index("head")
    rows = query_rows.shape[0]
    heads = HEADS // H
    pairs = heads // 2
    mine = lax.dynamic_slice_in_dim(block_lists[:, 0], me * heads, heads)
    tile = lax.axis_index("seq")
    counts = lax.dynamic_slice(block_counts, (me * heads, tile, 0), (heads, 1, S))
    lists = jnp.concatenate(
        [jnp.transpose(mine, (1, 0, 2)).reshape(S, heads * MOST), jnp.transpose(counts[:, 0])],
        axis=1,
    )
    lists = jnp.pad(lists, ((0, 0), (0, 128 - heads * (MOST + 1))))[:, None]
    bf16 = jnp.bfloat16
    piece = math.gcd(rows, BLOCK)
    pieces = (rows // piece, piece, query_rows.shape[1])
    tile_buffers = [
        pltpu.VMEM((TILE // piece, piece, 2 * DH), bf16) for _ in range(2 * pairs)
    ] + [pltpu.VMEM((TILE, 2 * DH), bf16) for _ in range(pairs)]
    anywhere = pl.BlockSpec(memory_space=pl.ANY)
    return pl.pallas_call(
        functools.partial(body, (H, S, rows, heads, piece)),
        out_shape=jax.ShapeDtypeStruct(query_rows.shape, bf16),
        in_specs=[anywhere] * 4,
        out_specs=anywhere,
        scratch_shapes=tile_buffers
        + [
            pltpu.VMEM((pairs, H, rows, 2 * DH), bf16),
            pltpu.VMEM((pairs, S - 1, 2, PAIR_MOST, BLOCK, DH), bf16),
            pltpu.VMEM((pairs, S - 1, 2, PAIR_MOST, BLOCK, DH), bf16),
            pltpu.VMEM((S - 1, 1, 128), jnp.int32),
            pltpu.SMEM((S - 1, 1, 128), jnp.int32),
            pltpu.SMEM((S, 1, 128), jnp.int32),
            pltpu.SemaphoreType.DMA((3, pairs, H)),
            pltpu.SemaphoreType.DMA((3, pairs, H)),
            pltpu.SemaphoreType.DMA((pairs, S - 1, 2)),
            pltpu.SemaphoreType.DMA((pairs, S - 1, 2)),
            pltpu.SemaphoreType.DMA((S - 1,)),
            pltpu.SemaphoreType.DMA((S - 1,)),
            pltpu.SemaphoreType.DMA((2,)),
            pltpu.SemaphoreType.DMA((pairs, H)),
            pltpu.SemaphoreType.DMA((pairs, H)),
        ],
        compiler_params=pltpu.CompilerParams(
            collective_id=0, has_side_effects=True, vmem_limit_bytes=60 << 20
        ),
        name="block_attention",
    )(lists, query_rows, key_rows.reshape(pieces), value_rows.reshape(pieces))


def solution(mesh):
    in_specs = (
        P(("parts", "seq", "head"), None),
        P(("parts", "seq", "head"), None),
        P(("parts", "seq", "head"), None),
        P("parts", "seq", None, None),
        P("parts", None, None),
    )
    out_specs = P(("parts", "seq", "head"), None)
    return jax.shard_map(
        on_device, mesh=mesh, in_specs=in_specs, out_specs=out_specs, check_vma=False
    )
```

profile of v0, /device:TPU:0, one launch (start us, length us, event | category | flops | bytes accessed | tf_op | source)
XLA Modules:
  0.0 114.1 jit_solution(15976443026410225614)
XLA Ops:
  0.0 0.0 copy-start
  0.0 0.7 copy-done
  0.7 0.1 dynamic-slice_bitcast_fusion.1
  0.8 0.8 dynamic-slice_bitcast_fusion
  1.5 0.1 copy.7
  1.6 0.1 reshape.10
  1.7 0.1 pad_add_fusion
  1.8 0.6 pad.4
  2.4 109.0 %block_attention.1 = bf16[192,4096]{1,0:T(8,128)(2,1)} custom-call(s32[4,1,128]{2,1,0:T(1,128)} %bitcast.13, bf16[192,4096]{1,0:T(8,128)(2,1)} %q_ref.1, bf16[3,64,4096]{2,1,0:T(8,128)(2,1)} %bitcast.11, bf16[3,64,4096]{2,1,0:T(8,128)(2,1)} %bitcast.12), custom_call_target="tpu_custom_call" | custom-call | tf_op jit(solution)/shard_map/block_attention/pallas_call | solution.py:264
  111.4 2.7 %copy.9 = bf16[192,4096]{1,0:T(8,128)(2,1)} copy(bf16[192,4096]{1,0:T(8,128)(2,1)} %block_attention.1) | data formatting | bytes 3145728
Async XLA Ops:
  0.0 0.7 copy-start
where the time goes:
time: 114 us
  Pallas kernels  109 us (96%)
  local copies, waits for them, and re-layouts  5.01 us (4%)
    pallas_call x1, Pallas kernels, on_device(): pl.pallas_call(functools.partial(body, (H, S, rows, heads, piece)), out_s...  109 us
    unnamed x3, local copies, waits for them, and re-layouts  3.4 us

commit v1 on v0

v1 whole, which is shorter than its diff:
```python
import functools
import math

import jax
import jax.numpy as jnp
from jax import lax
from jax.experimental import pallas as pl
from jax.experimental.pallas import tpu as pltpu
from jax.sharding import PartitionSpec as P

HEADS = 32
DH = 128
BLOCK = 128
MOST = 3
PAIR_MOST = 4
TILE = 768
MESH = pl.DeviceIdType.MESH


def contract_last(a, b):
    return lax.dot_general(a, b, (((1,), (1,)), ((), ())), preferred_element_type=jnp.float32)


def slot_ranges(p, c, pairs):
    if c == 1 and p == pairs - 1:
        return [(0, MOST), (MOST, PAIR_MOST)]
    if p == 0:
        return [(0, 1), (1, PAIR_MOST)]
    return [(0, PAIR_MOST)]


def body(dims, lists_ref, counts_ref, q_ref, k_ref, v_ref, out_ref, *scratch):
    H, S, rows, heads, piece = dims
    pairs = heads // 2
    last = pairs - 1
    chips = H // 2
    kb, vb, qb = scratch[: 2 * pairs], scratch[2 * pairs : 4 * pairs], scratch[4 * pairs : 5 * pairs]
    (ob, pk, fk, pbuf, mbuf, tbuf, lbuf, lsm, csm, x_send, x_recv, z_send, z_recv, l_send, l_recv, l_loc, o_send, o_recv) = (
        scratch[5 * pairs :]
    )
    me = lax.axis_index("head")
    tile = lax.axis_index("seq")

    def peer_of(i):
        chip = lax.rem(lax.div(me, 2) + 1 + lax.div(i, 2), chips)
        return chip * 2 + lax.rem(me + i + 1, 2)

    def source_of(i):
        chip = lax.rem(lax.div(me, 2) + 2 * chips - 1 - lax.div(i, 2), chips)
        return chip * 2 + lax.rem(me + i + 1, 2)

    def tile_after(d):
        return lax.rem(tile + d, S)

    def i32(i):
        return jnp.int32(i)

    counts_copy = pltpu.make_async_copy(counts_ref, csm, l_loc.at[0])
    counts_copy.start()
    barrier = pltpu.get_barrier_semaphore()
    for d in range(1, S):
        pl.semaphore_signal(barrier, inc=1, device_id={"seq": tile_after(d)}, device_id_type=MESH)
    for i in range(H - 1):
        pl.semaphore_signal(barrier, inc=1, device_id={"head": peer_of(i32(i))}, device_id_type=MESH)

    sources = (k_ref, v_ref, q_ref)

    def head_columns(owner, p, hs):
        return pl.ds(pl.multiple_of((owner * heads + 2 * p + hs) * DH, DH), DH)

    def pair_columns(owner, p):
        return pl.ds(pl.multiple_of((owner * heads + 2 * p) * DH, 2 * DH), 2 * DH)

    def row_range(owner):
        return pl.ds(pl.multiple_of(owner * rows, 16), rows)

    def source_at(a, owner, p, hs):
        if a == 2:
            return q_ref.at[:, pair_columns(owner, p)]
        return sources[a].at[:, :, head_columns(owner, p, hs)]

    def place_at(a, owner, p, hs):
        if a == 2:
            return qb[p].at[row_range(owner), :]
        held = (kb, vb)[a][2 * p + hs]
        return held.at[pl.ds(owner * (rows // piece), rows // piece)]

    def own_copy(a, p, hs):
        return pltpu.make_async_copy(source_at(a, me, p, hs), place_at(a, me, p, hs), x_recv.at[a, p, hs, H - 1])

    def x_copy(a, p, hs, i, landed):
        to = peer_of(i32(i))
        at = source_of(i32(i)) if landed else me
        return pltpu.make_async_remote_copy(
            src_ref=source_at(a, to, p, hs),
            dst_ref=place_at(a, at, p, hs),
            send_sem=x_send.at[a, p, hs, i],
            recv_sem=x_recv.at[a, p, hs, i],
            device_id={"head": to},
            device_id_type=MESH,
        )

    def l_copy(d):
        return pltpu.make_async_remote_copy(
            src_ref=lists_ref,
            dst_ref=lbuf.at[d - 1],
            send_sem=l_send.at[d - 1],
            recv_sem=l_recv.at[d - 1],
            device_id={"seq": tile_after(d)},
            device_id_type=MESH,
        )

    def z_copy(p, d, c, g):
        lo, hi = slot_ranges(p, c, pairs)[g]
        return pltpu.make_async_remote_copy(
            src_ref=pk.at[p, d - 1, c, lo:hi],
            dst_ref=fk.at[p, d - 1, c, lo:hi],
            send_sem=z_send.at[p, d - 1, c, g],
            recv_sem=z_recv.at[p, d - 1, c, g],
            device_id={"seq": tile_after(d)},
            device_id_type=MESH,
        )

    def o_copy(p, hs, i, landed):
        to = peer_of(i)
        at = source_of(i) if landed else me
        return pltpu.make_async_remote_copy(
            src_ref=ob.at[p, hs, i],
            dst_ref=out_ref.at[:, head_columns(at, p, hs)],
            send_sem=o_send.at[p, hs, i],
            recv_sem=o_recv.at[p, hs, i],
            device_id={"head": to},
            device_id_type=MESH,
        )

    def o_own(p, hs):
        return pltpu.make_async_copy(
            ob.at[p, hs, H - 1], out_ref.at[:, head_columns(me, p, hs)], o_recv.at[p, hs, H - 1]
        )

    def x_start(a, p):
        for hs in range(1 if a == 2 else 2):
            for i in range(H - 1):
                x_copy(a, p, hs, i, False).start()
            own_copy(a, p, hs).start()

    def x_arrived(a, p, hs):
        own_copy(a, p, hs).wait()
        for i in range(H - 1):
            x_copy(a, p, hs, i, True).wait_recv()

    pl.semaphore_wait(barrier, H - 1 + S - 1)
    order = []
    for p in range(pairs):
        order += [(0, p), (1, p)]
        if p >= 1:
            order.append((2, p - 1))
    order.append((2, last))
    early = order[:4]
    x_start(*early[0])
    for d in range(1, S):
        l_copy(d).start()
    for a, p in early[1:]:
        x_start(a, p)

    counts_copy.wait()
    for d in range(1, S):
        l_copy(d).wait_recv()
    to_scalars = pltpu.make_async_copy(lbuf, lsm, l_loc.at[1])
    to_scalars.start()
    to_scalars.wait()

    waited = set()

    def need(a, p, hs):
        if (a, p, hs) not in waited:
            waited.add((a, p, hs))
            x_arrived(a, p, hs)

    def pack(p, c, g):
        held = (kb, vb)[c][2 * p : 2 * p + 2]
        lo, hi = slot_ranges(p, c, pairs)[g]
        if lo < MOST:
            need(c, p, 0)
        if hi > 1:
            need(c, p, 1)
        head = me * heads + 2 * p
        for d in range(1, S):
            at = S - d - 1
            first = csm[tile_after(d), tile, head]
            for s in range(lo, hi):
                left = lsm[at, min(s, MOST - 1), tile, head]
                right = lsm[at, min(PAIR_MOST - 1 - s, MOST - 1), tile, head + 1]
                for b in range(BLOCK // piece):
                    if s < MOST:
                        chosen = held[0][left * (BLOCK // piece) + b]
                    if s > 0:
                        other = held[1][right * (BLOCK // piece) + b]
                        chosen = jnp.where(s < first, chosen, other) if s < MOST else other
                    pk[p, d - 1, c, s, pl.ds(b * piece, piece), :] = chosen
            z_copy(p, d, c, g).start()

    for p in range(pairs):
        for c in range(2):
            for g in range(len(slot_ranges(p, c, pairs))):
                pack(p, c, g)
        if p == 0:
            for a, pp in order[4:]:
                x_start(a, pp)

    factor = math.log2(math.e) / math.sqrt(DH)
    width = MOST * BLOCK
    lane = lax.broadcasted_iota(jnp.int32, (1, width), 1)

    def z_arrived(p, c, g):
        for d in range(1, S):
            z_copy(p, d, c, g).wait_recv()

    def scores_of(p, hs, q):
        scores = [contract_last(q, kb[2 * p + hs][...].reshape(TILE, DH))]
        for d in range(1, S):
            used = csm[tile, lax.rem(tile + S - d, S), me * heads + 2 * p + hs] * BLOCK
            live = lane < used if hs == 0 else lane >= width - used
            bias = jnp.where(live, 0.0, -jnp.inf).astype(jnp.float32)
            far = fk[p, d - 1, 0, hs : hs + MOST].reshape(width, DH)
            scores.append(contract_last(q, far) + bias)
        top = functools.reduce(jnp.maximum, [jnp.max(s, axis=1, keepdims=True) for s in scores])
        return scores, top

    def weigh(s, top):
        return jnp.exp2((s - top) * factor)

    def mix(w, v):
        return jnp.dot(w, v, preferred_element_type=jnp.float32)

    for p in range(last):
        need(2, p, 0)
        for c in range(2):
            for g in range(len(slot_ranges(p, c, pairs))):
                z_arrived(p, c, g)

        def chunk(i, carry, p=p):
            mine = row_range(peer_of(i))
            for hs in range(2):
                q = qb[p][mine, hs * DH : (hs + 1) * DH]
                scores, top = scores_of(p, hs, q)
                values = [vb[2 * p + hs][...].reshape(TILE, DH)]
                values += [fk[p, d - 1, 1, hs : hs + MOST].reshape(width, DH) for d in range(1, S)]
                total = jnp.zeros((rows, 1), jnp.float32)
                mixed = jnp.zeros((rows, DH), jnp.float32)
                for s, v in zip(scores, values):
                    w = weigh(s, top)
                    total = total + jnp.sum(w, axis=1, keepdims=True)
                    mixed = mixed + mix(w.astype(jnp.bfloat16), v)
                ob[p, hs, i] = (mixed / total).astype(jnp.bfloat16)

                @pl.when(i < H - 1)
                def _(hs=hs):
                    o_copy(p, hs, i, False).start()

            return carry

        lax.fori_loop(0, H, chunk, 0)
        for hs in range(2):
            o_own(p, hs).start()

    need(2, last, 0)
    for g in range(len(slot_ranges(last, 0, pairs))):
        z_arrived(last, 0, g)

    def weights_chunk(i, carry):
        mine = row_range(peer_of(i))
        for hs in range(2):
            q = qb[last][mine, hs * DH : (hs + 1) * DH]
            scores, top = scores_of(last, hs, q)
            w = weigh(scores[0], top)
            total = jnp.sum(w, axis=1, keepdims=True)
            mbuf[hs, i] = mix(w.astype(jnp.bfloat16), vb[2 * last + hs][...].reshape(TILE, DH))
            for d in range(1, S):
                w = weigh(scores[d], top)
                total = total + jnp.sum(w, axis=1, keepdims=True)
                pbuf[hs, i, :, (d - 1) * width : d * width] = w.astype(jnp.bfloat16)
            tbuf[hs, i] = total
        return carry

    lax.fori_loop(0, H, weights_chunk, 0)
    for hs in range(2):
        z_arrived(last, 1, hs)

        def values_chunk(i, carry, hs=hs):
            mixed = mbuf[hs, i]
            for d in range(1, S):
                v = fk[last, d - 1, 1, hs : hs + MOST].reshape(width, DH)
                mixed = mixed + mix(pbuf[hs, i, :, (d - 1) * width : d * width], v)
            ob[last, hs, i] = (mixed / tbuf[hs, i]).astype(jnp.bfloat16)

            @pl.when(i < H - 1)
            def _():
                o_copy(last, hs, i, False).start()

            return carry

        lax.fori_loop(0, H, values_chunk, 0)
        o_own(last, hs).start()

    for p in range(pairs):
        for hs in range(2):
            o_own(p, hs).wait()
            for i in range(H - 1):
                o_copy(p, hs, i32(i), True).wait_recv()
    for d in range(1, S):
        l_copy(d).wait_send()
        for p in range(pairs):
            for c in range(2):
                for g in range(len(slot_ranges(p, c, pairs))):
                    z_copy(p, d, c, g).wait_send()
    for p in range(pairs):
        for i in range(H - 1):
            for a in range(3):
                for hs in range(1 if a == 2 else 2):
                    x_copy(a, p, hs, i, False).wait_send()
            for hs in range(2):
                o_copy(p, hs, i32(i), False).wait_send()


def on_device(query_rows, key_rows, value_rows, block_lists, block_counts):
    H = lax.axis_size("head")
    S = lax.axis_size("seq")
    rows = query_rows.shape[0]
    heads = HEADS // H
    pairs = heads // 2
    lists = jnp.transpose(block_lists, (1, 3, 2, 0))[0]
    counts = jnp.transpose(block_counts, (1, 2, 0))
    bf16 = jnp.bfloat16
    piece = math.gcd(rows, BLOCK)
    pieces = (rows // piece, piece, query_rows.shape[1])
    hbm = pl.BlockSpec(memory_space=pltpu.HBM)
    return pl.pallas_call(
        functools.partial(body, (H, S, rows, heads, piece)),
        out_shape=pltpu.VMEM(query_rows.shape, bf16),
        in_specs=[hbm] * 5,
        out_specs=pl.BlockSpec(memory_space=pl.ANY),
        scratch_shapes=[pltpu.VMEM((TILE // piece, piece, DH), bf16) for _ in range(4 * pairs)]
        + [pltpu.VMEM((TILE, 2 * DH), bf16) for _ in range(pairs)]
        + [
            pltpu.VMEM((pairs, 2, H, rows, DH), bf16),
            pltpu.VMEM((pairs, S - 1, 2, PAIR_MOST, BLOCK, DH), bf16),
            pltpu.VMEM((pairs, S - 1, 2, PAIR_MOST, BLOCK, DH), bf16),
            pltpu.VMEM((2, H, rows, (S - 1) * MOST * BLOCK), bf16),
            pltpu.VMEM((2, H, rows, DH), jnp.float32),
            pltpu.VMEM((2, H, rows, 1), jnp.float32),
            pltpu.VMEM((S - 1,) + lists.shape, jnp.int32),
            pltpu.SMEM((S - 1,) + lists.shape, jnp.int32),
            pltpu.SMEM(counts.shape, jnp.int32),
            pltpu.SemaphoreType.DMA((3, pairs, 2, H)),
            pltpu.SemaphoreType.DMA((3, pairs, 2, H)),
            pltpu.SemaphoreType.DMA((pairs, S - 1, 2, 2)),
            pltpu.SemaphoreType.DMA((pairs, S - 1, 2, 2)),
            pltpu.SemaphoreType.DMA((S - 1,)),
            pltpu.SemaphoreType.DMA((S - 1,)),
            pltpu.SemaphoreType.DMA((2,)),
            pltpu.SemaphoreType.DMA((pairs, 2, H)),
            pltpu.SemaphoreType.DMA((pairs, 2, H)),
        ],
        compiler_params=pltpu.CompilerParams(
            collective_id=0, has_side_effects=True, vmem_limit_bytes=60 << 20
        ),
        name="block_attention",
    )(lists, counts, query_rows, key_rows.reshape(pieces), value_rows.reshape(pieces))


def solution(mesh):
    in_specs = (
        P(("parts", "seq", "head"), None),
        P(("parts", "seq", "head"), None),
        P(("parts", "seq", "head"), None),
        P("parts", "seq", None, None),
        P("parts", None, None),
    )
    out_specs = P(("parts", "seq", "head"), None)
    return jax.shard_map(
        on_device, mesh=mesh, in_specs=in_specs, out_specs=out_specs, check_vma=False
    )
```

time: 114 us -> 110 us (0.965)
  local copies, waits for them, and re-layouts: 5.01 us -> 1.15 us
    unnamed x3 -> x1, local copies, waits for them, and re-layouts: 3.4 us -> 1.15 us
where the time goes in v1:
time: 110 us; the launch traced here: 109 us
  Pallas kernels  108 us (98%)
  local copies, waits for them, and re-layouts  1.15 us (1%)
    pallas_call x1, Pallas kernels, on_device(): pl.pallas_call(functools.partial(body, (H, S, rows, heads, piece)), out_s...  108 us

profile of v1, /device:TPU:0, one launch (start us, length us, event | category | flops | bytes accessed | tf_op | source)
XLA Modules:
  0.0 109.5 jit_solution(15124001483513870276)
XLA Ops:
  0.0 108.3 %block_attention.1 = bf16[192,4096]{1,0:T(8,128)(2,1)S(1)} custom-call(s32[3,4,32]{2,1,0:T(4,128)} %bitcast.9, s32[4,4,32]{2,1,0:T(4,128)} %bitcast.8, bf16[192,4096]{1,0:T(8,128)(2,1)} %q_ref.1, bf16[3,64,4096]{2,1,0:T(8,128)(2,1)} %bitcast.6, bf16[3,64,4096]{2,1,0:T(8,128)(2,1)} %bitcast.7), custom_call_target="tpu_custom_call" | custom-call | tf_op jit(solution)/shard_map/block_attention/pallas_call | solution.py:338
  108.3 1.1 %copy.7 = bf16[192,4096]{1,0:T(8,128)(2,1)} copy(bf16[192,4096]{1,0:T(8,128)(2,1)S(1)} %block_attention.1) | data formatting | bytes 3145728

commit v2 on v1

v2 whole, which is shorter than its diff:
```python
import functools
import math

import jax
import jax.numpy as jnp
from jax import lax
from jax.experimental import pallas as pl
from jax.experimental.pallas import tpu as pltpu
from jax.sharding import PartitionSpec as P

HEADS = 32
DH = 128
BLOCK = 128
MOST = 3
PAIR_MOST = 4
TILE = 768
MESH = pl.DeviceIdType.MESH
ROOMS = (1, PAIR_MOST)
VMEM_LIMIT = 60 << 20


def contract_last(a, b):
    return lax.dot_general(a, b, (((1,), (1,)), ((), ())), preferred_element_type=jnp.float32)


def rank_at(H, pairs, h, p):
    if pairs != 4:
        return p * H + h
    chips = H // 2
    if p == 2:
        return 2 * H + lax.rem(h, 2) * chips + lax.div(h, 2)
    return {0: 0, 1: 3 * H, 3: H}[p] + h


def heavy_pairs(H, pairs):
    return 2 * H + H // 2 if pairs == 4 else H * pairs


def ranked(counts, H, pairs):
    total = HEADS // 2
    f32 = jnp.float32
    head_no = lax.broadcasted_iota(jnp.int32, (HEADS, total), 0)
    pair_no = lax.broadcasted_iota(jnp.int32, (HEADS, total), 1)
    in_pair = jnp.where((head_no == 2 * pair_no) | (head_no == 2 * pair_no + 1), 1.0, 0.0).astype(f32)
    most = jnp.zeros((1, total), f32)
    for t in range(counts.shape[0]):
        sums = jnp.dot(counts[t].astype(f32), in_pair, preferred_element_type=f32)
        most = jnp.maximum(most, jnp.max(sums, axis=0, keepdims=True))
    row = lax.broadcasted_iota(jnp.int32, (total, total), 0)
    col = lax.broadcasted_iota(jnp.int32, (total, total), 1)
    along = jnp.broadcast_to(most, (total, total))
    down = jnp.sum(jnp.where(row == col, along, 0.0), axis=1, keepdims=True)
    ahead = (along > down) | ((along == down) & (col < row))
    rank = jnp.sum(jnp.where(ahead, 1.0, 0.0), axis=1, keepdims=True)
    pair_at = jnp.sum(jnp.where(rank == col.astype(f32), row.astype(f32), 0.0), axis=0, keepdims=True)
    rank_of = jnp.sum(jnp.where(row == col, jnp.broadcast_to(rank, (total, total)), 0.0), axis=0, keepdims=True)
    room = jnp.sum(jnp.where(rank == float(heavy_pairs(H, pairs)), down, 0.0), axis=0, keepdims=True)
    return rank_of, pair_at, room


def survey_body(dims, counts_ref, info_ref, pick_ref, own, others, load, send, recv):
    NP, H, pairs = dims
    total = HEADS // 2
    part = lax.axis_index("parts")
    barrier = pltpu.get_barrier_semaphore()
    for d in range(1, NP):
        pl.semaphore_signal(barrier, inc=1, device_id={"parts": lax.rem(part + d, NP)}, device_id_type=MESH)
    mine = pltpu.make_async_copy(counts_ref, own, load.at[0])
    mine.start()

    def copy(d):
        return pltpu.make_async_remote_copy(
            src_ref=counts_ref,
            dst_ref=others.at[d - 1],
            send_sem=send.at[d - 1],
            recv_sem=recv.at[d - 1],
            device_id={"parts": lax.rem(part + d, NP)},
            device_id_type=MESH,
        )

    pl.semaphore_wait(barrier, NP - 1)
    for d in range(1, NP):
        copy(d).start()
    mine.wait()
    rank_of, pair_at, room = ranked(own, H, pairs)
    info_ref[0:1, :total] = pair_at.astype(jnp.int32)
    info_ref[1:2, :total] = rank_of.astype(jnp.int32)
    for d in range(1, NP):
        copy(d).wait_recv()
        room = jnp.maximum(room, ranked(others.at[d - 1], H, pairs)[2])
    pick = jnp.zeros((1, 1), jnp.int32)
    for less in ROOMS[:-1]:
        pick = pick + (room > float(less)).astype(jnp.int32)
    pick_ref[...] = pick
    for d in range(1, NP):
        copy(d).wait_send()


def survey(counts, NP, H, pairs):
    return pl.pallas_call(
        functools.partial(survey_body, (NP, H, pairs)),
        out_shape=(jax.ShapeDtypeStruct((8, 128), jnp.int32), jax.ShapeDtypeStruct((1, 1), jnp.int32)),
        in_specs=[pl.BlockSpec(memory_space=pltpu.HBM)],
        out_specs=(pl.BlockSpec(memory_space=pltpu.VMEM),) * 2,
        scratch_shapes=[
            pltpu.VMEM(counts.shape, jnp.int32),
            pltpu.VMEM((NP - 1,) + counts.shape, jnp.int32),
            pltpu.SemaphoreType.DMA((1,)),
            pltpu.SemaphoreType.DMA((NP - 1,)),
            pltpu.SemaphoreType.DMA((NP - 1,)),
        ],
        compiler_params=pltpu.CompilerParams(collective_id=0, has_side_effects=True),
        name="survey",
    )(counts)


def slot_ranges(p, c, pairs, room):
    if c == 1 and p == pairs - 1:
        return [(0, MOST), (MOST, room)]
    if p == 0:
        return [(0, 1), (1, room)]
    return [(0, room)]


def body(dims, lists_ref, counts_ref, info_ref, q_ref, k_ref, v_ref, out_ref, *scratch):
    H, S, rows, heads, piece, light = dims
    pairs = heads // 2
    last = pairs - 1
    chips = H // 2
    kb, vb, qb = scratch[: 2 * pairs], scratch[2 * pairs : 4 * pairs], scratch[4 * pairs : 5 * pairs]
    (qin, kin, vin, qs, ks, vs, ob, land, pk, fk, pbuf, mbuf, tbuf, lbuf, lsm, csm, info,
     x_send, x_recv, z_send, z_recv, l_send, l_recv, l_loc, o_send, o_recv) = scratch[5 * pairs :]
    me = lax.axis_index("head")
    tile = lax.axis_index("seq")
    core = lax.rem(me, 2)

    def peer_of(i):
        chip = lax.rem(lax.div(me, 2) + 1 + lax.div(i, 2), chips)
        return chip * 2 + lax.rem(me + i + 1, 2)

    def source_of(i):
        chip = lax.rem(lax.div(me, 2) + 2 * chips - 1 - lax.div(i, 2), chips)
        return chip * 2 + lax.rem(me + i + 1, 2)

    def tile_after(d):
        return lax.rem(tile + d, S)

    def i32(i):
        return jnp.int32(i)

    def with_room(p, what):
        if pairs != 4 or light == PAIR_MOST or p in (0, last):
            what(PAIR_MOST)
        elif p == 1:
            what(light)
        else:
            pl.when(core == 0)(lambda: what(PAIR_MOST))
            pl.when(core != 0)(lambda: what(light))

    scalars = [
        pltpu.make_async_copy(ref, to, l_loc.at[n])
        for n, (ref, to) in enumerate(((info_ref, info), (counts_ref, csm)))
    ]
    inputs = ((k_ref, kin), (v_ref, vin), (q_ref, qin))
    scalars[0].start()
    scalars[1].start()
    for a, (ref, to) in enumerate(inputs):
        for pair in range(HEADS // 2):
            columns = slice(2 * pair * DH, 2 * (pair + 1) * DH)
            pltpu.make_async_copy(ref.at[..., columns], to.at[pair], l_loc.at[2 + a]).start()
    barrier = pltpu.get_barrier_semaphore()
    for d in range(1, S):
        pl.semaphore_signal(barrier, inc=1, device_id={"seq": tile_after(d)}, device_id_type=MESH)
    for i in range(H - 1):
        pl.semaphore_signal(barrier, inc=1, device_id={"head": peer_of(i32(i))}, device_id_type=MESH)

    def pair_of(h, p):
        return info[0, rank_at(H, pairs, h, p)]

    def row_range(owner):
        return pl.ds(pl.multiple_of(owner * rows, 16), rows)

    def piece_range(owner):
        return pl.ds(owner * (rows // piece), rows // piece)

    def staged(a, p, hs, i):
        return qs.at[p, i] if a == 2 else (ks, vs)[a].at[p, hs, i]

    def place_at(a, owner, p, hs):
        if a == 2:
            return qb[p].at[row_range(owner), :]
        return (kb, vb)[a][2 * p + hs].at[piece_range(owner)]

    def x_copy(a, p, hs, i, landed):
        at = source_of(i32(i)) if landed else me
        return pltpu.make_async_remote_copy(
            src_ref=staged(a, p, hs, i),
            dst_ref=place_at(a, at, p, hs),
            send_sem=x_send.at[a],
            recv_sem=x_recv.at[a, p, hs],
            device_id={"head": peer_of(i32(i))},
            device_id_type=MESH,
        )

    def l_copy(d):
        return pltpu.make_async_remote_copy(
            src_ref=lists_ref,
            dst_ref=lbuf.at[d - 1],
            send_sem=l_send.at[0],
            recv_sem=l_recv.at[0],
            device_id={"seq": tile_after(d)},
            device_id_type=MESH,
        )

    def z_copy(p, d, c, g, room):
        lo, hi = slot_ranges(p, c, pairs, room)[g]
        return pltpu.make_async_remote_copy(
            src_ref=pk.at[p, d - 1, c, lo:hi],
            dst_ref=fk.at[p, d - 1, c, lo:hi],
            send_sem=z_send.at[p],
            recv_sem=z_recv.at[p, c, g],
            device_id={"seq": tile_after(d)},
            device_id_type=MESH,
        )

    def o_copy(p, hs, i, landed):
        at = source_of(i) if landed else me
        return pltpu.make_async_remote_copy(
            src_ref=ob.at[p, hs, i],
            dst_ref=land.at[rank_at(H, pairs, at, p), hs],
            send_sem=o_send.at[0],
            recv_sem=o_recv.at[0],
            device_id={"head": peer_of(i)},
            device_id_type=MESH,
        )

    loaded = set()

    def x_start(a, p):
        if a not in loaded:
            loaded.add(a)
            whole = inputs[a][1]
            pltpu.make_async_copy(whole, whole, l_loc.at[2 + a]).wait()
        for hs in range(1 if a == 2 else 2):
            for i in range(H):
                pair = pair_of(peer_of(i32(i)), p)
                if a == 2:
                    taken = qin[pair]
                else:
                    taken = (kin, vin)[a][pair, :, :, hs * DH : (hs + 1) * DH]
                if i < H - 1:
                    staged(a, p, hs, i)[...] = taken
                    x_copy(a, p, hs, i, False).start()
                else:
                    place_at(a, me, p, hs)[...] = taken

    def all_of(ref, send_sem, recv_sem):
        return pltpu.make_async_remote_copy(
            src_ref=ref, dst_ref=ref, send_sem=send_sem, recv_sem=recv_sem,
            device_id={"head": peer_of(i32(0))}, device_id_type=MESH,
        )

    def x_arrived(a, p, hs):
        all_of(qs.at[p] if a == 2 else (ks, vs)[a].at[p, hs], x_send.at[a], x_recv.at[a, p, hs]).wait_recv()

    scalars[0].wait()
    pl.semaphore_wait(barrier, H - 1 + S - 1)
    for d in range(1, S):
        l_copy(d).start()
    order = []
    for p in range(pairs):
        order += [(0, p), (1, p)]
        if p >= 1:
            order.append((2, p - 1))
    order.append((2, last))
    for a, p in order[:4]:
        x_start(a, p)

    scalars[1].wait()
    all_of(lbuf, l_send.at[0], l_recv.at[0]).wait_recv()
    to_scalars = pltpu.make_async_copy(lbuf, lsm, l_loc.at[5])
    to_scalars.start()
    to_scalars.wait()

    waited = set()

    def need(a, p, hs):
        if (a, p, hs) not in waited:
            waited.add((a, p, hs))
            x_arrived(a, p, hs)

    def pack(p, c, g, room):
        held = (kb, vb)[c][2 * p : 2 * p + 2]
        lo, hi = slot_ranges(p, c, pairs, room)[g]
        most = min(MOST, room)
        head = 2 * pair_of(me, p)
        for d in range(1, S):
            at = S - d - 1
            first = csm[tile_after(d), tile, head]
            for s in range(lo, hi):
                left = lsm[at, min(s, MOST - 1), tile, head]
                right = lsm[at, min(room - 1 - s, MOST - 1), tile, head + 1]
                for b in range(BLOCK // piece):
                    if s < most:
                        chosen = held[0][left * (BLOCK // piece) + b]
                    if s >= room - most:
                        other = held[1][right * (BLOCK // piece) + b]
                        chosen = jnp.where(s < first, chosen, other) if s < most else other
                    pk[p, d - 1, c, s, pl.ds(b * piece, piece), :] = chosen
            z_copy(p, d, c, g, room).start()

    def pack_place(p, c):
        if p == 0:
            need(c, p, 0)
            pack(p, c, 0, PAIR_MOST)
            need(c, p, 1)
            for g in range(1, len(slot_ranges(p, c, pairs, PAIR_MOST))):
                pack(p, c, g, PAIR_MOST)
        else:
            need(c, p, 0)
            need(c, p, 1)

            def send(room):
                for g in range(len(slot_ranges(p, c, pairs, room))):
                    pack(p, c, g, room)

            with_room(p, send)

    factor = math.log2(math.e) / math.sqrt(DH)

    def z_arrived(p, c, g, room):
        lo, hi = slot_ranges(p, c, pairs, room)[g]
        all_of(fk.at[p, :, c, lo:hi], z_send.at[p], z_recv.at[p, c, g]).wait_recv()

    def far_slots(hs, room):
        most = min(MOST, room)
        return slice(0, most) if hs == 0 else slice(room - most, room)

    def far_blocks(p, c, d, hs, room):
        return fk[p, d - 1, c, far_slots(hs, room)].reshape(min(MOST, room) * BLOCK, DH)

    def scores_of(p, hs, q, room):
        width = min(MOST, room) * BLOCK
        lane = lax.broadcasted_iota(jnp.int32, (1, width), 1)
        scores = [contract_last(q, kb[2 * p + hs][...].reshape(TILE, DH))]
        head = 2 * pair_of(me, p) + hs
        for d in range(1, S):
            used = csm[tile, lax.rem(tile + S - d, S), head] * BLOCK
            live = lane < used if hs == 0 else lane >= width - used
            bias = jnp.where(live, 0.0, -jnp.inf).astype(jnp.float32)
            scores.append(contract_last(q, far_blocks(p, 0, d, hs, room)) + bias)
        top = functools.reduce(jnp.maximum, [jnp.max(s, axis=1, keepdims=True) for s in scores])
        return scores, top

    def weigh(s, top):
        return jnp.exp2((s - top) * factor)

    def mix(w, v):
        return jnp.dot(w, v, preferred_element_type=jnp.float32)

    def finish(p, hs, i, out):
        ob[p, hs, i] = out

        @pl.when(i < H - 1)
        def _():
            o_copy(p, hs, i, False).start()

    def land_own(p, hs):
        land[rank_at(H, pairs, me, p), hs] = ob[p, hs, H - 1]

    def weigh_place(p):
        def all_chunks(room):
            width = min(MOST, room) * BLOCK
            for g in range(len(slot_ranges(p, 0, pairs, room))):
                z_arrived(p, 0, g, room)

            def chunk(i, carry):
                mine = row_range(peer_of(i))
                for hs in range(2):
                    q = qb[p][mine, hs * DH : (hs + 1) * DH]
                    scores, top = scores_of(p, hs, q, room)
                    w = weigh(scores[0], top)
                    total = jnp.sum(w, axis=1, keepdims=True)
                    mbuf[hs, i] = mix(w.astype(jnp.bfloat16), vb[2 * p + hs][...].reshape(TILE, DH))
                    for d in range(1, S):
                        w = weigh(scores[d], top)
                        total = total + jnp.sum(w, axis=1, keepdims=True)
                        pbuf[hs, i, :, (d - 1) * width : d * width] = w.astype(jnp.bfloat16)
                    tbuf[hs, i] = total
                return carry

            lax.fori_loop(0, H, chunk, 0)

        need(2, p, 0)
        with_room(p, all_chunks)

    def mix_place(p):
        def all_chunks(room):
            width = min(MOST, room) * BLOCK
            groups = len(slot_ranges(p, 1, pairs, room))
            for hs in range(2):
                for g in range(groups) if p < last and hs == 0 else range(hs, hs + 1) if p == last else ():
                    z_arrived(p, 1, g, room)

                def chunk(i, carry, hs=hs):
                    mixed = mbuf[hs, i]
                    for d in range(1, S):
                        weights = pbuf[hs, i, :, (d - 1) * width : d * width]
                        mixed = mixed + mix(weights, far_blocks(p, 1, d, hs, room))
                    finish(p, hs, i, (mixed / tbuf[hs, i]).astype(jnp.bfloat16))
                    return carry

                lax.fori_loop(0, H, chunk, 0)
                land_own(p, hs)

        with_room(p, all_chunks)

    pack_place(0, 0)
    pack_place(0, 1)
    for a, p in order[4:]:
        x_start(a, p)
    for p in range(1, last):
        pack_place(p, 0)
        pack_place(p, 1)
    for p in range(pairs):
        weigh_place(p)
        mix_place(p)
        if last > 0 and p < 2:
            for c in range(2) if last == 1 else (p,):
                if p < last:
                    pack_place(last, c)

    sent_out = all_of(ob.at[:, :, : H - 1], o_send.at[0], o_recv.at[0])
    sent_out.wait_recv()
    for pair in range(HEADS // 2):
        rank = info[1, pair]
        for hs in range(2):
            out_ref[:, (2 * pair + hs) * DH : (2 * pair + hs + 1) * DH] = land[rank, hs]
    all_of(lbuf, l_send.at[0], l_recv.at[0]).wait_send()
    for p in range(pairs):

        def sent(room, p=p):
            all_of(pk.at[p, :, :, :room], z_send.at[p], z_recv.at[p, 0, 0]).wait_send()

        with_room(p, sent)
    for a, ref in enumerate((ks, vs, qs)):
        all_of(ref, x_send.at[a], x_recv.at[a, 0, 0]).wait_send()
    sent_out.wait_send()


def attention(dims, number, lists, counts, info, query_rows, key_rows, value_rows):
    H, S, rows, heads, piece, light = dims
    pairs = heads // 2
    bf16 = jnp.bfloat16
    chunk = (rows // piece, piece, query_rows.shape[1])
    operands = (lists, counts, info, query_rows, key_rows.reshape(chunk), value_rows.reshape(chunk))
    return pl.pallas_call(
        functools.partial(body, dims),
        out_shape=pltpu.VMEM(query_rows.shape, bf16),
        in_specs=[pl.BlockSpec(memory_space=pltpu.HBM)] * 6,
        out_specs=pl.BlockSpec(memory_space=pltpu.VMEM),
        scratch_shapes=[pltpu.VMEM((TILE // piece, piece, DH), bf16) for _ in range(4 * pairs)]
        + [pltpu.VMEM((TILE, 2 * DH), bf16) for _ in range(pairs)]
        + [
            pltpu.VMEM((HEADS // 2, rows, 2 * DH), bf16),
            pltpu.VMEM((HEADS // 2, rows // piece, piece, 2 * DH), bf16),
            pltpu.VMEM((HEADS // 2, rows // piece, piece, 2 * DH), bf16),
            pltpu.VMEM((pairs, H - 1, rows, 2 * DH), bf16),
            pltpu.VMEM((pairs, 2, H - 1, rows // piece, piece, DH), bf16),
            pltpu.VMEM((pairs, 2, H - 1, rows // piece, piece, DH), bf16),
            pltpu.VMEM((pairs, 2, H, rows, DH), bf16),
            pltpu.VMEM((HEADS // 2, 2, rows, DH), bf16),
            pltpu.VMEM((pairs, S - 1, 2, PAIR_MOST, BLOCK, DH), bf16),
            pltpu.VMEM((pairs, S - 1, 2, PAIR_MOST, BLOCK, DH), bf16),
            pltpu.VMEM((2, H, rows, (S - 1) * MOST * BLOCK), bf16),
            pltpu.VMEM((2, H, rows, DH), jnp.float32),
            pltpu.VMEM((2, H, rows, 1), jnp.float32),
            pltpu.VMEM((S - 1,) + lists.shape, jnp.int32),
            pltpu.SMEM((S - 1,) + lists.shape, jnp.int32),
            pltpu.SMEM(counts.shape, jnp.int32),
            pltpu.SMEM((8, 128), jnp.int32),
            pltpu.SemaphoreType.DMA((3,)),
            pltpu.SemaphoreType.DMA((3, pairs, 2)),
            pltpu.SemaphoreType.DMA((pairs,)),
            pltpu.SemaphoreType.DMA((pairs, 2, 2)),
            pltpu.SemaphoreType.DMA((1,)),
            pltpu.SemaphoreType.DMA((1,)),
            pltpu.SemaphoreType.DMA((6,)),
            pltpu.SemaphoreType.DMA((1,)),
            pltpu.SemaphoreType.DMA((1,)),
        ],
        compiler_params=pltpu.CompilerParams(
            collective_id=number, has_side_effects=True, vmem_limit_bytes=VMEM_LIMIT
        ),
        name=f"block_attention_{light}",
    )(*operands)


def on_device(query_rows, key_rows, value_rows, block_lists, block_counts):
    H = lax.axis_size("head")
    S = lax.axis_size("seq")
    rows = query_rows.shape[0]
    heads = HEADS // H
    pairs = heads // 2
    lists = jnp.transpose(block_lists, (1, 3, 2, 0))[0]
    counts = jnp.transpose(block_counts, (1, 2, 0))
    piece = math.gcd(rows, BLOCK)
    rooms = ROOMS if pairs == 4 else (PAIR_MOST,)
    kernels = [
        functools.partial(attention, (H, S, rows, heads, piece, room), 1 + n) for n, room in enumerate(rooms)
    ]
    if len(rooms) == 1:
        info = jnp.broadcast_to(jnp.arange(128, dtype=jnp.int32), (8, 128))
        return kernels[0](lists, counts, info, query_rows, key_rows, value_rows)
    info, pick = survey(counts, lax.axis_size("parts"), H, pairs)
    return lax.switch(pick[0, 0], kernels, lists, counts, info, query_rows, key_rows, value_rows)


def solution(mesh):
    in_specs = (
        P(("parts", "seq", "head"), None),
        P(("parts", "seq", "head"), None),
        P(("parts", "seq", "head"), None),
        P("parts", "seq", None, None),
        P("parts", None, None),
    )
    out_specs = P(("parts", "seq", "head"), None)
    return jax.shard_map(
        on_device, mesh=mesh, in_specs=in_specs, out_specs=out_specs, check_vma=False
    )
```

time: 110 us -> 89.4 us (0.81)
  Pallas kernels: 108 us -> 87.3 us
    pallas_call x1 -> x2, Pallas kernels: 108 us -> 87.3 us  [the longest x1 81.5 us: attention(): pl.pallas_call(functools.partial(body, dims), out_shape=pltpu.VMEM(query_...]
where the time goes in v2:
time: 89.4 us; the launch traced here: 89.2 us
  Pallas kernels  87.3 us (98%)
  local copies, waits for them, and re-layouts  1.15 us (1%)
    pallas_call x1, Pallas kernels, attention(): pl.pallas_call(functools.partial(body, dims), out_shape=pltpu.VMEM(query_...  81.5 us
    pallas_call x1, Pallas kernels, survey(): pl.pallas_call(functools.partial(survey_body, (NP, H, pairs)), out_shape=...  5.73 us

profile of v2, /device:TPU:0, one launch (start us, length us, event | category | flops | bytes accessed | tf_op | source)
XLA Modules:
  0.0 89.2 jit_solution(8525138581416392739)
XLA Ops:
  0.0 5.7 %survey.1 = (s32[8,128]{1,0:T(8,128)S(1)}, s32[1,1]{1,0:T(1,128)}) custom-call(s32[4,4,32]{2,1,0:T(4,128)} %bitcast.13), custom_call_target="tpu_custom_call" | custom-call | tf_op jit(solution)/shard_map/survey/pallas_call | solution.py:100
  6.3 81.7 %conditional.1 = (bf16[192,4096]{1,0:T(8,128)(2,1)S(1)}) conditional(s32[]{:T(128)} %bitcast.7, (bf16[192,4096]{1,0:T(8,128)(2,1)}, bf16[192,4096]{1,0:T(8,128)(2,1)}, s32[1,3,4,32]{3,2,1,0:T(4,128)}, s32[4,4,32]{2,1,0:T(4,128)}, s32[8,128]{1,0:T(8,128)S(1)}, /*index=5*/bf16[192,4096]{1,0:T(8,128)(2,1)}) %tuple.18, (bf16[192,4096]{1,0:T(8,128)(2,1)}, ...), branch_computations={%region_0.0_spmd, %region_1.0_spmd} | conditional | bytes 8 | solution.py:516
  6.4 81.5 %block_attention_1.1 = bf16[192,4096]{1,0:T(8,128)(2,1)S(1)} custom-call(s32[3,4,32]{2,1,0:T(4,128)} %bitcast.18, s32[4,4,32]{2,1,0:T(4,128)} %get-tuple-element.33.counts_ref, s32[8,128]{1,0:T(8,128)S(1)} %get-tuple-element.34.info_ref, bf16[192,4096]{1,0:T(8,128)(2,1)} %get-tuple-element.61.q_ref, bf16[3,64,4096]{2,1,0:T(8,128)(2,1)} %bitcast.9, ...), custom_call_target="tpu_custom_call" | custom-call | tf_op jit(solution)/shard_map/cond/branch_0_fun/block_attention_1/pallas_call | solution.py:457
  88.1 1.1 %copy.17 = bf16[192,4096]{1,0:T(8,128)(2,1)} copy(bf16[192,4096]{1,0:T(8,128)(2,1)S(1)} %get-tuple-element.48) | data formatting | bytes 3145728

commit v3 on v2

--- a/solution.py
+++ b/solution.py
@@ -267,12 +267,10 @@
     pl.semaphore_wait(barrier, H - 1 + S - 1)
     for d in range(1, S):
         l_copy(d).start()
-    order = []
-    for p in range(pairs):
-        order += [(0, p), (1, p)]
-        if p >= 1:
-            order.append((2, p - 1))
-    order.append((2, last))
+    if pairs == 4:
+        order = [(0, 0), (1, 0), (0, 1), (1, 1), (2, 0), (0, 2), (0, 3), (1, 2), (2, 1), (2, 2), (1, 3), (2, 3)]
+    else:
+        order = [(a, p) for p in range(pairs) for a in range(3)]
     for a, p in order[:4]:
         x_start(a, p)
 
@@ -381,12 +379,12 @@
                     scores, top = scores_of(p, hs, q, room)
                     w = weigh(scores[0], top)
                     total = jnp.sum(w, axis=1, keepdims=True)
-                    mbuf[hs, i] = mix(w.astype(jnp.bfloat16), vb[2 * p + hs][...].reshape(TILE, DH))
+                    mbuf[p % 2, hs, i] = mix(w.astype(jnp.bfloat16), vb[2 * p + hs][...].reshape(TILE, DH))
                     for d in range(1, S):
                         w = weigh(scores[d], top)
                         total = total + jnp.sum(w, axis=1, keepdims=True)
-                        pbuf[hs, i, :, (d - 1) * width : d * width] = w.astype(jnp.bfloat16)
-                    tbuf[hs, i] = total
+                        pbuf[p % 2, hs, i, :, (d - 1) * width : d * width] = w.astype(jnp.bfloat16)
+                    tbuf[p % 2, hs, i] = total
                 return carry
 
             lax.fori_loop(0, H, chunk, 0)
@@ -403,11 +401,11 @@
                     z_arrived(p, 1, g, room)
 
                 def chunk(i, carry, hs=hs):
-                    mixed = mbuf[hs, i]
+                    mixed = mbuf[p % 2, hs, i]
                     for d in range(1, S):
-                        weights = pbuf[hs, i, :, (d - 1) * width : d * width]
+                        weights = pbuf[p % 2, hs, i, :, (d - 1) * width : d * width]
                         mixed = mixed + mix(weights, far_blocks(p, 1, d, hs, room))
-                    finish(p, hs, i, (mixed / tbuf[hs, i]).astype(jnp.bfloat16))
+                    finish(p, hs, i, (mixed / tbuf[p % 2, hs, i]).astype(jnp.bfloat16))
                     return carry
 
                 lax.fori_loop(0, H, chunk, 0)
@@ -419,16 +417,28 @@
     pack_place(0, 1)
     for a, p in order[4:]:
         x_start(a, p)
-    for p in range(1, last):
-        pack_place(p, 0)
-        pack_place(p, 1)
-    for p in range(pairs):
-        weigh_place(p)
-        mix_place(p)
-        if last > 0 and p < 2:
-            for c in range(2) if last == 1 else (p,):
-                if p < last:
-                    pack_place(last, c)
+    if pairs == 4:
+        pack_place(1, 0)
+        pack_place(1, 1)
+        pack_place(2, 0)
+        pack_place(3, 0)
+        weigh_place(0)
+        mix_place(0)
+        pack_place(2, 1)
+        weigh_place(1)
+        mix_place(1)
+        weigh_place(2)
+        pack_place(3, 1)
+        weigh_place(3)
+        mix_place(2)
+        mix_place(3)
+    else:
+        for p in range(1, pairs):
+            pack_place(p, 0)
+            pack_place(p, 1)
+        for p in range(pairs):
+            weigh_place(p)
+            mix_place(p)
 
     sent_out = all_of(ob.at[:, :, : H - 1], o_send.at[0], o_recv.at[0])
     sent_out.wait_recv()
@@ -472,9 +482,9 @@
             pltpu.VMEM((HEADS // 2, 2, rows, DH), bf16),
             pltpu.VMEM((pairs, S - 1, 2, PAIR_MOST, BLOCK, DH), bf16),
             pltpu.VMEM((pairs, S - 1, 2, PAIR_MOST, BLOCK, DH), bf16),
-            pltpu.VMEM((2, H, rows, (S - 1) * MOST * BLOCK), bf16),
-            pltpu.VMEM((2, H, rows, DH), jnp.float32),
-            pltpu.VMEM((2, H, rows, 1), jnp.float32),
+            pltpu.VMEM((min(2, pairs), 2, H, rows, (S - 1) * MOST * BLOCK), bf16),
+            pltpu.VMEM((min(2, pairs), 2, H, rows, DH), jnp.float32),
+            pltpu.VMEM((min(2, pairs), 2, H, rows, 1), jnp.float32),
             pltpu.VMEM((S - 1,) + lists.shape, jnp.int32),
             pltpu.SMEM((S - 1,) + lists.shape, jnp.int32),
             pltpu.SMEM(counts.shape, jnp.int32),

time: 89.4 us -> 87.1 us (0.974)
  Pallas kernels: 87.3 us -> 85 us
    pallas_call x1, Pallas kernels: 81.5 us -> 79.2 us  [attention(): pl.pallas_call(functools.partial(body, dims), out_shape=pltpu.VMEM(query_...]
where the time goes in v3:
time: 87.1 us; the launch traced here: 86.9 us
  Pallas kernels  85 us (98%)
  local copies, waits for them, and re-layouts  1.15 us (1%)
    pallas_call x1, Pallas kernels, attention(): pl.pallas_call(functools.partial(body, dims), out_shape=pltpu.VMEM(query_...  79.2 us
    pallas_call x1, Pallas kernels, survey(): pl.pallas_call(functools.partial(survey_body, (NP, H, pairs)), out_shape=...  5.73 us

profile of v3, /device:TPU:0, one launch (start us, length us, event | category | flops | bytes accessed | tf_op | source)
XLA Modules:
  0.0 86.9 jit_solution(12448542553216081920)
XLA Ops:
  0.0 5.7 %survey.1 = (s32[8,128]{1,0:T(8,128)S(1)}, s32[1,1]{1,0:T(1,128)}) custom-call(s32[4,4,32]{2,1,0:T(4,128)} %bitcast.13), custom_call_target="tpu_custom_call" | custom-call | tf_op jit(solution)/shard_map/survey/pallas_call | solution.py:100
  6.3 79.4 %conditional.1 = (bf16[192,4096]{1,0:T(8,128)(2,1)S(1)}) conditional(s32[]{:T(128)} %bitcast.7, (bf16[192,4096]{1,0:T(8,128)(2,1)}, bf16[192,4096]{1,0:T(8,128)(2,1)}, s32[1,3,4,32]{3,2,1,0:T(4,128)}, s32[4,4,32]{2,1,0:T(4,128)}, s32[8,128]{1,0:T(8,128)S(1)}, /*index=5*/bf16[192,4096]{1,0:T(8,128)(2,1)}) %tuple.18, (bf16[192,4096]{1,0:T(8,128)(2,1)}, ...), branch_computations={%region_0.0_spmd, %region_1.0_spmd} | conditional | bytes 8 | solution.py:526
  6.4 79.2 %block_attention_1.1 = bf16[192,4096]{1,0:T(8,128)(2,1)S(1)} custom-call(s32[3,4,32]{2,1,0:T(4,128)} %bitcast.18, s32[4,4,32]{2,1,0:T(4,128)} %get-tuple-element.33.counts_ref, s32[8,128]{1,0:T(8,128)S(1)} %get-tuple-element.34.info_ref, bf16[192,4096]{1,0:T(8,128)(2,1)} %get-tuple-element.61.q_ref, bf16[3,64,4096]{2,1,0:T(8,128)(2,1)} %bitcast.9, ...), custom_call_target="tpu_custom_call" | custom-call | tf_op jit(solution)/shard_map/cond/branch_0_fun/block_attention_1/pallas_call | solution.py:467
  85.8 1.1 %copy.17 = bf16[192,4096]{1,0:T(8,128)(2,1)} copy(bf16[192,4096]{1,0:T(8,128)(2,1)S(1)} %get-tuple-element.48) | data formatting | bytes 3145728

commit v4 on v3

--- a/solution.py
+++ b/solution.py
@@ -15,7 +15,7 @@
 PAIR_MOST = 4
 TILE = 768
 MESH = pl.DeviceIdType.MESH
-ROOMS = (1, PAIR_MOST)
+ROOMS = (1, 2, PAIR_MOST)
 VMEM_LIMIT = 60 << 20
 
 
@@ -157,6 +157,12 @@
             pl.when(core == 0)(lambda: what(PAIR_MOST))
             pl.when(core != 0)(lambda: what(light))
 
+    barrier = pltpu.get_barrier_semaphore()
+    for d in range(1, S):
+        pl.semaphore_signal(barrier, inc=1, device_id={"seq": tile_after(d)}, device_id_type=MESH)
+    for i in range(H - 1):
+        pl.semaphore_signal(barrier, inc=1, device_id={"head": peer_of(i32(i))}, device_id_type=MESH)
+
     scalars = [
         pltpu.make_async_copy(ref, to, l_loc.at[n])
         for n, (ref, to) in enumerate(((info_ref, info), (counts_ref, csm)))
@@ -168,12 +174,6 @@
         for pair in range(HEADS // 2):
             columns = slice(2 * pair * DH, 2 * (pair + 1) * DH)
             pltpu.make_async_copy(ref.at[..., columns], to.at[pair], l_loc.at[2 + a]).start()
-    barrier = pltpu.get_barrier_semaphore()
-    for d in range(1, S):
-        pl.semaphore_signal(barrier, inc=1, device_id={"seq": tile_after(d)}, device_id_type=MESH)
-    for i in range(H - 1):
-        pl.semaphore_signal(barrier, inc=1, device_id={"head": peer_of(i32(i))}, device_id_type=MESH)
-
     def pair_of(h, p):
         return info[0, rank_at(H, pairs, h, p)]
 

time: 87.1 us -> 87.1 us (level)
  no operation moved by 1% of the time
where the time goes in v4:
time: 87.1 us; the launch traced here: 86.9 us
  Pallas kernels  84.9 us (97%)
  local copies, waits for them, and re-layouts  1.15 us (1%)
    pallas_call x1, Pallas kernels, attention(): pl.pallas_call(functools.partial(body, dims), out_shape=pltpu.VMEM(query_...  79.2 us
    pallas_call x1, Pallas kernels, survey(): pl.pallas_call(functools.partial(survey_body, (NP, H, pairs)), out_shape=...  5.71 us

profile of v4, /device:TPU:0, one launch (start us, length us, event | category | flops | bytes accessed | tf_op | source)
XLA Modules:
  0.0 86.9 jit_solution(7971353175951536485)
XLA Ops:
  0.0 5.7 %survey.1 = (s32[8,128]{1,0:T(8,128)S(1)}, s32[1,1]{1,0:T(1,128)}) custom-call(s32[4,4,32]{2,1,0:T(4,128)} %bitcast.18), custom_call_target="tpu_custom_call" | custom-call | tf_op jit(solution)/shard_map/survey/pallas_call | solution.py:100
  6.3 79.4 %conditional.1 = (bf16[192,4096]{1,0:T(8,128)(2,1)S(1)}) conditional(s32[]{:T(128)} %bitcast.10, (bf16[192,4096]{1,0:T(8,128)(2,1)}, bf16[192,4096]{1,0:T(8,128)(2,1)}, s32[1,3,4,32]{3,2,1,0:T(4,128)}, s32[4,4,32]{2,1,0:T(4,128)}, s32[8,128]{1,0:T(8,128)S(1)}, /*index=5*/bf16[192,4096]{1,0:T(8,128)(2,1)}) %tuple.24, ...), branch_computations={%region_0.0_spmd, %region_1.0_spmd, %region_2.0_spmd} | conditional | bytes 8 | solution.py:526
  6.3 79.2 %block_attention_1.1 = bf16[192,4096]{1,0:T(8,128)(2,1)S(1)} custom-call(s32[3,4,32]{2,1,0:T(4,128)} %bitcast.25, s32[4,4,32]{2,1,0:T(4,128)} %get-tuple-element.46.counts_ref, s32[8,128]{1,0:T(8,128)S(1)} %get-tuple-element.47.info_ref, bf16[192,4096]{1,0:T(8,128)(2,1)} %get-tuple-element.86.q_ref, bf16[3,64,4096]{2,1,0:T(8,128)(2,1)} %bitcast.12, ...), custom_call_target="tpu_custom_call" | custom-call | tf_op jit(solution)/shard_map/cond/branch_0_fun/block_attention_1/pallas_call | solution.py:467
  85.8 1.1 %copy.22 = bf16[192,4096]{1,0:T(8,128)(2,1)} copy(bf16[192,4096]{1,0:T(8,128)(2,1)S(1)} %get-tuple-element.67) | data formatting | bytes 3145728

commit v5 on v4

--- a/solution.py
+++ b/solution.py
@@ -205,7 +205,7 @@
     def l_copy(d):
         return pltpu.make_async_remote_copy(
             src_ref=lists_ref,
-            dst_ref=lbuf.at[d - 1],
+            dst_ref=lsm.at[d - 1],
             send_sem=l_send.at[0],
             recv_sem=l_recv.at[0],
             device_id={"seq": tile_after(d)},
@@ -275,10 +275,7 @@
         x_start(a, p)
 
     scalars[1].wait()
-    all_of(lbuf, l_send.at[0], l_recv.at[0]).wait_recv()
-    to_scalars = pltpu.make_async_copy(lbuf, lsm, l_loc.at[5])
-    to_scalars.start()
-    to_scalars.wait()
+    all_of(lsm, l_send.at[0], l_recv.at[0]).wait_recv()
 
     waited = set()
 
@@ -446,7 +443,7 @@
         rank = info[1, pair]
         for hs in range(2):
             out_ref[:, (2 * pair + hs) * DH : (2 * pair + hs + 1) * DH] = land[rank, hs]
-    all_of(lbuf, l_send.at[0], l_recv.at[0]).wait_send()
+    all_of(lsm, l_send.at[0], l_recv.at[0]).wait_send()
     for p in range(pairs):
 
         def sent(room, p=p):

time: 87.1 us -> 86.7 us (level)
  no operation moved by 1% of the time
where the time goes in v5:
time: 86.7 us; the launch traced here: 86.6 us
  Pallas kernels  84.6 us (98%)
  local copies, waits for them, and re-layouts  1.15 us (1%)
    pallas_call x1, Pallas kernels, attention(): pl.pallas_call(functools.partial(body, dims), out_shape=pltpu.VMEM(query_...  78.9 us
    pallas_call x1, Pallas kernels, survey(): pl.pallas_call(functools.partial(survey_body, (NP, H, pairs)), out_shape=...  5.71 us

profile of v5, /device:TPU:0, one launch (start us, length us, event | category | flops | bytes accessed | tf_op | source)
XLA Modules:
  0.0 86.6 jit_solution(13948214903749668566)
XLA Ops:
  0.0 5.7 %survey.1 = (s32[8,128]{1,0:T(8,128)S(1)}, s32[1,1]{1,0:T(1,128)}) custom-call(s32[4,4,32]{2,1,0:T(4,128)} %bitcast.18), custom_call_target="tpu_custom_call" | custom-call | tf_op jit(solution)/shard_map/survey/pallas_call | solution.py:100
  6.3 79.1 %conditional.1 = (bf16[192,4096]{1,0:T(8,128)(2,1)S(1)}) conditional(s32[]{:T(128)} %bitcast.10, (bf16[192,4096]{1,0:T(8,128)(2,1)}, bf16[192,4096]{1,0:T(8,128)(2,1)}, s32[1,3,4,32]{3,2,1,0:T(4,128)}, s32[4,4,32]{2,1,0:T(4,128)}, s32[8,128]{1,0:T(8,128)S(1)}, /*index=5*/bf16[192,4096]{1,0:T(8,128)(2,1)}) %tuple.24, ...), branch_computations={%region_0.0_spmd, %region_1.0_spmd, %region_2.0_spmd} | conditional | bytes 8 | solution.py:523
  6.3 78.9 %block_attention_1.1 = bf16[192,4096]{1,0:T(8,128)(2,1)S(1)} custom-call(s32[3,4,32]{2,1,0:T(4,128)} %bitcast.25, s32[4,4,32]{2,1,0:T(4,128)} %get-tuple-element.46.counts_ref, s32[8,128]{1,0:T(8,128)S(1)} %get-tuple-element.47.info_ref, bf16[192,4096]{1,0:T(8,128)(2,1)} %get-tuple-element.86.q_ref, bf16[3,64,4096]{2,1,0:T(8,128)(2,1)} %bitcast.12, ...), custom_call_target="tpu_custom_call" | custom-call | tf_op jit(solution)/shard_map/cond/branch_0_fun/block_attention_1/pallas_call | solution.py:464
  85.4 1.1 %copy.22 = bf16[192,4096]{1,0:T(8,128)(2,1)} copy(bf16[192,4096]{1,0:T(8,128)(2,1)S(1)} %get-tuple-element.67) | data formatting | bytes 3145728
